TPU v7x, 32 devices: a whole 2x2x4 slice. The times are simulated.
32 devices in a mesh: row: 8 (over z, y), col: 4 (over x, core).
Axes of the slice: x: 2, y: 2, z: 4, core: 2. Of those that a mesh axis runs over, the one named last changes fastest.
Arguments:
- load_currents: float32 [32, 1024, 512], P(None, 'row', 'col'), may hold values from -36 to 36
- labels: int32 [1024, 512], P('row', 'col'), may hold values from 0 to 255, as said below
- bump_height: float32 [1024, 512], P('row', 'col'), may hold values from 0.5 to 2
- horizontal_class: int32 [1024, 512], P('row', 'col'), may hold values from 0 to 7
- vertical_class: int32 [1024, 512], P('row', 'col'), may hold values from 0 to 7
- pad_class: int32 [1024, 512], P('row', 'col'), may hold values from 0 to 7
- edge_table: float32 [8], replicated, may hold values from 0.5 to 4
- pad_table: float32 [8], replicated, may hold values from 0.02 to 0.5
Outputs:
- solution: float32 [32, 1024, 512], P(None, 'row', 'col')
- residual: float32 [32, 1024, 512], P(None, 'row', 'col')
Inputs may be any that keep to these rules, and one draw needn't show every extreme that they name: `labels`: every number from 0 to 255 is the label of some nodes; the label of node (i, j) is 16 * floor(16 * i2 / 1024) + floor(16 * j2 / 512) for some node (i2, j2) of the grid with |i2 - i| <= 16 and |j2 - j| <= 8.
All inputs are finite; a program needn't handle non-finite values.
Results may differ from a plain program's by a relative error of at most 0.0003.
Values sent between devices are 32-bit elements; how exact they have to be, the bound alone decides.
A program may use at most 128 MiB of HBM per device.

v0:
```python
import jax
import jax.numpy as jnp
from jax import lax
from jax.sharding import PartitionSpec as P

REG = 16
ITERS = 2
precise = lax.Precision.HIGHEST


def from_behind(value, axis, steps):
    count = lax.axis_size(axis)
    initial, last = (max(0, -steps), min(count, count - steps))
    return lax.ppermute(value, axis, [(source, source + steps) for source in range(initial, last)])


def extended(value, sides, width):
    for axis, dim in sides:
        size, length = (lax.axis_size(axis), value.shape[dim])
        up = [(i, (i + 1) % size) for i in range(size - 1)]
        down = [(j, i) for i, j in up]
        last = lax.slice_in_dim(value, length - width, length, axis=dim)
        initial = lax.slice_in_dim(value, 0, width, axis=dim)
        before = lax.ppermute(last, axis, up)
        after = lax.ppermute(initial, axis, down)
        value = jnp.concatenate([before, value, after], axis=dim)
    return value


def lookup(entries, classes):
    levels = lax.broadcasted_iota(jnp.int32, (entries.shape[0],) + classes.shape, 0)
    return jnp.sum(jnp.where(classes[None] == levels, entries[:, None, None], 0.0), axis=0)


def stencil(padded, coeffs):
    diagonal, right_link, left_link, down_link, upper_link = coeffs
    centre = padded[:, 1:-1, 1:-1]
    return (
        diagonal * centre
        - right_link * padded[:, 1:-1, 2:]
        - left_link * padded[:, 1:-1, :-2]
        - down_link * padded[:, 2:, 1:-1]
        - upper_link * padded[:, :-2, 1:-1]
    )


def invert(matrix):
    factor = jnp.linalg.cholesky(matrix)
    identity = jnp.eye(matrix.shape[0], dtype=matrix.dtype)
    lower_solved = lax.linalg.triangular_solve(factor, identity, left_side=True, lower=True)
    return lax.linalg.triangular_solve(
        factor, lower_solved, left_side=True, lower=True, transpose_a=True
    )


def body(
    load_currents,
    labels,
    bump_height,
    horizontal_class,
    vertical_class,
    pad_class,
    edge_table,
    pad_table,
):
    tile_rows, tile_cols = labels.shape
    regions = REG * REG
    load_count = load_currents.shape[0]
    tile_cells = tile_rows * tile_cols
    grid_rows = lax.axis_size("row") * tile_rows
    grid_cols = lax.axis_size("col") * tile_cols
    row_ids = lax.axis_index("row") * tile_rows + lax.broadcasted_iota(jnp.int32, labels.shape, 0)
    col_ids = lax.axis_index("col") * tile_cols + lax.broadcasted_iota(jnp.int32, labels.shape, 1)
    right_link = jnp.where(col_ids == grid_cols - 1, 0.0, lookup(edge_table, horizontal_class))
    down_link = jnp.where(row_ids == grid_rows - 1, 0.0, lookup(edge_table, vertical_class))
    left_edge = from_behind(right_link[:, -1:], "col", 1)
    left_link = jnp.concatenate([left_edge, right_link[:, :-1]], axis=1)
    upper_edge = from_behind(down_link[-1:, :], "row", 1)
    upper_link = jnp.concatenate([upper_edge, down_link[:-1, :]], axis=0)
    diagonal = lookup(pad_table, pad_class) + right_link + left_link + down_link + upper_link
    coeffs = (diagonal, right_link, left_link, down_link, upper_link)
    levels = lax.broadcasted_iota(jnp.int32, (regions,) + labels.shape, 0)
    deflation = jnp.where(labels[None] == levels, bump_height[None], 0.0)
    deflation_image = stencil(extended(deflation, (("row", 1), ("col", 2)), 1), coeffs)
    basis_flat = deflation.reshape(regions, tile_cells)
    image_flat = deflation_image.reshape(regions, tile_cells)
    contract = (((1,), (1,)), ((), ()))
    partial_matrix = lax.dot_general(basis_flat, image_flat, contract, precision=precise)
    inverse = invert(lax.psum(partial_matrix, ("row", "col")))

    def project(field):
        return lax.dot_general(
            field.reshape(load_count, tile_cells), basis_flat, contract, precision=precise
        )

    def expand(coarse):
        return jnp.dot(coarse, basis_flat, precision=precise).reshape(
            load_count, tile_rows, tile_cols
        )

    def correction_image(coarse):
        return jnp.dot(coarse, image_flat, precision=precise).reshape(
            load_count, tile_rows, tile_cols
        )

    def refresh(residual):
        scaled = residual / diagonal
        local_norm = jnp.sum(residual * scaled, axis=(1, 2))
        field_image = stencil(extended(scaled, (("row", 1), ("col", 2)), 1), coeffs)
        weighted_norm = lax.psum(local_norm, ("row", "col"))
        projected = lax.psum(project(field_image), ("row", "col"))
        coarse = jnp.dot(projected, inverse, precision=precise)
        return (scaled, weighted_norm, field_image, coarse)

    load_sums = lax.psum(project(load_currents), ("row", "col"))
    coarse = jnp.dot(load_sums, inverse, precision=precise)
    solution = expand(coarse)
    residual = load_currents - correction_image(coarse)
    scaled, weighted_norm, field_image, coarse = refresh(residual)
    spread = expand(coarse)
    direction = scaled - spread
    direction_image = field_image - correction_image(coarse)
    for iteration in range(ITERS):
        local_curve = jnp.sum(direction * direction_image, axis=(1, 2))
        curvature = lax.psum(local_curve, ("row", "col"))
        step_size = (weighted_norm / curvature)[:, None, None]
        solution = solution + step_size * direction
        residual = residual - step_size * direction_image
        if iteration + 1 < ITERS:
            scaled, new_norm, field_image, coarse = refresh(residual)
            spread = expand(coarse)
            beta_ratio = (new_norm / weighted_norm)[:, None, None]
            direction = scaled - spread + beta_ratio * direction
            direction_image = field_image - correction_image(coarse) + beta_ratio * direction_image
            weighted_norm = new_norm
    return (solution, residual)


def solution(mesh):
    return jax.shard_map(
        body,
        mesh=mesh,
        in_specs=(
            P(None, "row", "col"),
            P("row", "col"),
            P("row", "col"),
            P("row", "col"),
            P("row", "col"),
            P("row", "col"),
            P(),
            P(),
        ),
        out_specs=(P(None, "row", "col"), P(None, "row", "col")),
        check_vma=False,
    )
```

profile of v0, /device:TPU:0, one launch (start us, length us, event | category | flops | bytes accessed | tf_op | source)
XLA Modules:
  0.0 716.1 jit_solution(5788398756781292680)
XLA Ops:
  7.2 1.1 select_reduce_fusion.1
  8.4 2.4 collective-permute-start
  11.0 4.4 collective-permute-start.1
  15.3 5.4 fusion.28
  20.8 3.4 collective-permute-start.2
  24.3 1.4 collective-permute-start.3
  25.7 18.0 %fusion.84 = f32[32,256]{1,0:T(8,128)S(1)} fusion(f32[32,128,128]{2,1,0:T(8,128)S(1)} %copy-done.11, f32[128,128]{1,0:T(8,128)S(1)} %copy-done.12, s32[128,128]{1,0:T(8,128)S(1)} %copy-done.13), kind=kOutput, calls=%fused_computation.114 | convolution fusion | flops 1619001344 | bytes 2260992 | tf_op jit(solution)/shard_map/dot_general | solution.py:92
  44.1 1.3 collective-permute-start.4
  45.4 3.8 collective-permute-start.5
  49.3 0.8 collective-permute-done.5
  50.1 31.3 %fusion.17 = f32[256,128,128]{0,2,1:T(8,128)S(1)} fusion(f32[256,128,128]{0,2,1:T(8,128)} %copy-done.1, f32[256,1,128]{0,2,1:T(8,128)S(1)} %collective-permute-done.2, f32[256,1,128]{0,2,1:T(8,128)S(1)} %collective-permute-done.3, f32[256,130,1]{0,2,1:T(1,128)S(1)} %collective-permute-done.5, f32[256,130,1]{0,2,1:T(1,128)S(1)} %collective-permute-done.4, ...), kind=kLoop, calls=%fused_computation.20 | loop fusion | flops 79691776 | bytes 34541568 | tf_op jit(solution)/shard_map/sub | solution.py:39
  81.5 5.7 copy-done
  87.2 38.4 %fusion.81 = f32[256,256]{0,1:T(8,128)} fusion(f32[256,128,128]{0,2,1:T(8,128)S(1)} %fusion.17, f32[128,128]{1,0:T(8,128)S(1)} %copy-done.12, s32[128,128]{1,0:T(8,128)S(1)} %copy-done.13), kind=kOutput, calls=%fused_computation.110 | convolution fusion | flops 12893290496 | bytes 17170432 | tf_op jit(solution)/shard_map/dot_general | solution.py:88
  125.7 45.2 %psum.56 = f32[32,256]{1,0:T(8,128)S(1)} all-reduce(f32[32,256]{1,0:T(8,128)S(1)} %fusion.84), channel_id=1, replica_groups=mesh['row'=8,'col'=4] {'row','col'}, use_global_device_ids=true, to_apply=%region_0.1 | all-reduce | flops 8192 | bytes 65536 | tf_op jit(solution)/shard_map/psum | solution.py:115
  170.9 87.1 %all-reduce.5.cloned.1.call-done = f32[256,256]{0,1:T(8,128)} async-done(((f32[256,256]{0,1:T(8,128)}), f32[256,256]{0,1:T(8,128)}) %all-reduce.5.cloned.1.call-update) | async-done | bytes 262160 | tf_op jit(solution)/shard_map/psum | solution.py:89
  258.0 1.1 copy.46
  259.1 1.0 fusion.95
  260.1 11.7 %cholesky.53 = f32[128,128]{1,0:T(8,128)S(1)} custom-call(f32[128,128]{1,0:T(8,128)S(1)} %cholesky.121), custom_call_target="Cholesky" | custom-call | tf_op jit(solution)/shard_map/jit(cholesky)/cholesky | solution.py:48
  271.9 9.8 %custom-call.16 = f32[1,128,128]{1,2,0:T(8,128)S(1)} custom-call(f32[1,128,128]{2,1,0:T(8,128)S(1)} %get-tuple-element.56), custom_call_target="InvertDiagBlocksLowerTriangular" | custom-call | tf_op jit(solution)/shard_map/jit(cholesky)/cholesky | solution.py:48
  282.2 11.7 %cholesky.108 = f32[128,128]{1,0:T(8,128)S(1)} custom-call(f32[128,128]{1,0:T(8,128)S(1)} %convolution_subtract_fusion.2), custom_call_target="Cholesky" | custom-call | tf_op jit(solution)/shard_map/jit(cholesky)/cholesky | solution.py:48
  296.1 4.1 while.1
  296.7 1.4 bitcast_dynamic-update-slice_fusion.2
  298.7 1.4 bitcast_dynamic-update-slice_fusion.2
  300.2 20.1 %custom-call.17 = f32[2,128,128]{1,2,0:T(8,128)S(1)} custom-call(f32[2,128,128]{2,1,0:T(8,128)S(1)} %get-tuple-element.9), custom_call_target="InvertDiagBlocksLowerTriangular" | custom-call | tf_op jit(solution)/shard_map/triangular_solve | solution.py:51
  322.2 18.5 %multiply_reduce_fusion.3 = (f32[32]{0:T(128)S(1)}, f32[32,128,128]{2,0,1:T(8,128)S(1)}, f32[32,128,128]{2,0,1:T(8,128)}) fusion(f32[128,128]{1,0:T(8,128)S(1)} %get-tuple-element.34, f32[32,256,1]{1,0,2:T(8,128)S(1)} %convolution_bitcast_fusion.2, f32[256,128,128]{0,2,1:T(8,128)} %copy-done, f32[32,128,128]{2,1,0:T(8,128)} %param.8), kind=kOutput, calls=%fused_computation.105 | convolution fusion | flops 1612709888 | bytes 23167104 | tf_op jit(solution)/shard_map/dot_general | solution.py:102
  340.7 3.4 collective-permute-start.6
  344.1 1.3 collective-permute-start.7
  345.5 4.2 collective-permute-done.7
  349.9 2.7 fusion.119
  352.7 3.2 copy.48
  355.9 1.3 collective-permute-start.8
  357.2 3.2 copy.50
  360.4 3.2 collective-permute-start.9
  363.6 3.6 copy.49
  367.1 3.6 copy.51
  370.7 4.6 fusion.59
  375.4 1.3 copy-done.10
  376.7 16.4 %fusion.89 = f32[32,256]{1,0:T(8,128)S(1)} fusion(f32[32,128,128]{2,0,1:T(8,128)S(1)} %fusion.59, f32[128,128]{1,0:T(8,128)S(1)} %copy-done.12, s32[128,128]{1,0:T(8,128)S(1)} %copy-done.13), kind=kOutput, calls=%fused_computation.115 | convolution fusion | flops 1619001344 | bytes 2260992 | tf_op jit(solution)/shard_map/dot_general | solution.py:92
  393.1 40.3 %psum.59 = f32[32,256]{1,0:T(8,128)S(1)} all-reduce(f32[32,256]{1,0:T(8,128)S(1)} %fusion.89), channel_id=1, replica_groups=mesh['row'=8,'col'=4] {'row','col'}, use_global_device_ids=true, to_apply=%region_11.12 | all-reduce | flops 8192 | bytes 65536 | tf_op jit(solution)/shard_map/psum | solution.py:111
  433.7 17.8 %fusion.76 = f32[32,128,128]{2,0,1:T(8,128)S(1)} fusion(f32[32,128,128]{2,0,1:T(8,128)} %copy-done.10, f32[32,256,1]{1,0,2:T(8,128)S(1)} %convolution_bitcast_fusion.1, f32[256,128,128]{0,2,1:T(8,128)} %copy-done), kind=kOutput, calls=%fused_computation.109 | convolution fusion | flops 1611137024 | bytes 21004288 | tf_op jit(solution)/shard_map/dot_general | solution.py:102
  451.6 20.1 %multiply_reduce_fusion.2 = (f32[32]{0:T(128)S(1)}, f32[32,128,128]{2,0,1:T(8,128)}) fusion(f32[32,128,128]{2,0,1:T(8,128)S(1)} %fusion.76, f32[32,256,1]{1,0,2:T(8,128)S(1)} %convolution_bitcast_fusion.1, f32[128,128]{1,0:T(8,128)S(1)} %copy-done.12, s32[128,128]{1,0:T(8,128)S(1)} %copy-done.13, f32[32,128,128]{2,0,1:T(8,128)S(1)} %copy-done.8, ...), kind=kOutput, calls=%fused_computation.104 | convolution fusion | flops 1621098496 | bytes 6520960 | tf_op jit(solution)/shard_map/dot_general | solution.py:97
  471.6 39.8 %all-reduce.2 = (f32[32]{0:T(128)S(1)}, f32[32]{0:T(128)S(1)}) all-reduce(f32[32]{0:T(128)S(1)} %get-tuple-element.43, f32[32]{0:T(128)S(1)} %get-tuple-element.60), channel_id=1, replica_groups=mesh['row'=8,'col'=4] {'row','col'}, use_global_device_ids=true, to_apply=%region_10.11 | all-reduce | flops 64 | bytes 512 | tf_op jit(solution)/shard_map/psum | solution.py:110
  511.5 2.4 multiply_reduce_fusion.1
  514.2 1.0 copy-done.4
  515.2 4.2 collective-permute-start.10
  519.4 1.5 collective-permute-start.11
  520.9 4.1 collective-permute-done.11
  525.2 2.7 fusion.118
  527.9 3.2 copy.53
  531.2 1.3 collective-permute-start.12
  532.5 3.2 copy.55
  535.7 3.0 collective-permute-start.13
  538.7 3.6 copy.54
  542.3 3.6 copy.56
  545.9 4.6 fusion.51
  550.5 16.5 %fusion.92 = f32[32,256]{1,0:T(8,128)S(1)} fusion(f32[32,128,128]{2,0,1:T(8,128)S(1)} %fusion.51, f32[128,128]{1,0:T(8,128)S(1)} %copy-done.12, s32[128,128]{1,0:T(8,128)S(1)} %copy-done.13), kind=kOutput, calls=%fused_computation.116 | convolution fusion | flops 1619001344 | bytes 2260992 | tf_op jit(solution)/shard_map/dot_general | solution.py:92
  567.0 40.7 %all-reduce.1 = (f32[32,256]{1,0:T(8,128)S(1)}, f32[32]{0:T(128)S(1)}) all-reduce(f32[32,256]{1,0:T(8,128)S(1)} %fusion.92, f32[32]{0:T(128)S(1)} %get-tuple-element.32), channel_id=1, replica_groups=mesh['row'=8,'col'=4] {'row','col'}, use_global_device_ids=true, to_apply=%region_16.17 | all-reduce | flops 8224 | bytes 65792 | tf_op jit(solution)/shard_map/psum | solution.py:111
  608.0 17.9 %multiply_add_fusion.1 = f32[32,128,128]{2,0,1:T(8,128)S(1)} fusion(f32[32,128,128]{2,0,1:T(8,128)S(1)} %copy-done.3, f32[32,128,128]{2,0,1:T(8,128)} %copy-done.9, f32[32,256,1]{1,0,2:T(8,128)S(1)} %convolution_bitcast_fusion, f32[256,128,128]{0,2,1:T(8,128)} %copy-done, f32[32]{0:T(128)S(1)} %div.37), kind=kOutput, calls=%fused_computation.100 | convolution fusion | flops 1612185600 | bytes 23101568 | tf_op jit(solution)/shard_map/dot_general | solution.py:102
  625.9 18.9 %multiply_reduce_fusion = (f32[32]{0:T(128)S(1)}, f32[32,128,128]{2,0,1:T(8,128)}) fusion(f32[32,128,128]{2,0,1:T(8,128)S(1)} %multiply_add_fusion.1, f32[32,128,128]{2,0,1:T(8,128)S(1)} %copy-done.16, f32[32]{0:T(128)S(1)} %div.37, f32[32,256,1]{1,0,2:T(8,128)S(1)} %convolution_bitcast_fusion, f32[128,128]{1,0:T(8,128)S(1)} %copy-done.12, ...), kind=kOutput, calls=%fused_computation.99 | convolution fusion | flops 1622147072 | bytes 8618240 | tf_op jit(solution)/shard_map/dot_general | solution.py:97
  644.8 39.4 %psum.63 = f32[32]{0:T(128)S(1)} all-reduce(f32[32]{0:T(128)S(1)} %get-tuple-element.62), channel_id=1, replica_groups=mesh['row'=8,'col'=4] {'row','col'}, use_global_device_ids=true, to_apply=%region_18.19 | all-reduce | flops 32 | bytes 256 | tf_op jit(solution)/shard_map/psum | solution.py:125
  684.2 2.1 multiply_subtract_fusion
  686.4 2.5 copy.59
  688.9 17.3 %multiply_add_fusion = f32[32,128,128]{2,0,1:T(8,128)S(1)} fusion(f32[32,128,128]{2,0,1:T(8,128)S(1)} %copy-done.18, f32[32,128,128]{2,0,1:T(8,128)S(1)} %copy-done.17, f32[32,256,1]{1,0,2:T(8,128)S(1)} %convolution_bitcast_fusion.2, f32[128,128]{1,0:T(8,128)S(1)} %copy-done.12, s32[128,128]{1,0:T(8,128)S(1)} %copy-done.13, f32[32]{0:T(128)S(1)} %div.38, ...), kind=kOutput, calls=%fused_computation.98 | convolution fusion | flops 1621098496 | bytes 6455552 | tf_op jit(solution)/shard_map/dot_general | solution.py:97
  706.2 2.5 copy.58
  (91 shorter events, 6.6 us)
Async XLA Ops:
  7.2 250.8 %all-reduce.5.cloned.1.call-start = ((), (), s32[]{:S(2)}) async-start(), calls=%async_computation | async-start | bytes 524288 | tf_op jit(solution)/shard_map/psum | solution.py:89
  8.4 40.8 %collective-permute-start = (f32[128,1]{1,0:T(8,128)S(1)}, f32[128,1]{1,0:T(8,128)S(1)}, u32[]{:S(2)}, u32[]{:S(2)}) collective-permute-start(f32[128,1]{1,0:T(8,128)S(1)} %slice.188), channel_id=1, source_target_pairs={{0,1},{1,2},{2,3},{4,5},{5,6},{6,7},{8,9},{9,10},{10,11},{12,13},{... | collective-permute-start | bytes 1544 | tf_op jit(solution)/shard_map/ppermute | solution.py:14
  10.9 14.8 %copy-start.11 = (f32[32,128,128]{2,1,0:T(8,128)S(1)}, f32[32,128,128]{2,1,0:T(8,128)}, u32[]{:S(2)}) copy-start(f32[32,128,128]{2,1,0:T(8,128)} %param.8) | copy-start | bytes 6291460
  10.9 14.8 %copy-start.12 = (f32[128,128]{1,0:T(8,128)S(1)}, f32[128,128]{1,0:T(8,128)}, u32[]{:S(2)}) copy-start(f32[128,128]{1,0:T(8,128)} %param.10) | copy-start | bytes 196612
  10.9 14.8 %copy-start.13 = (s32[128,128]{1,0:T(8,128)S(1)}, s32[128,128]{1,0:T(8,128)}, u32[]{:S(2)}) copy-start(s32[128,128]{1,0:T(8,128)} %param.9) | copy-start | bytes 196612
  11.0 38.2 %collective-permute-start.1 = (f32[1,128]{1,0:T(1,128)S(1)}, f32[1,128]{1,0:T(1,128)S(1)}, u32[]{:S(2)}, u32[]{:S(2)}) collective-permute-start(f32[1,128]{1,0:T(1,128)S(1)} %slice.190), channel_id=1, source_target_pairs={{0,4},{4,8},{8,12},{12,16},{16,20},{20,24},{24,28},{1,5},{5,9},{9,... | collective-permute-start | bytes 1544 | tf_op jit(solution)/shard_map/ppermute | solution.py:14
  20.7 23.2 %copy-start.1 = (f32[256,128,128]{0,2,1:T(8,128)}, f32[256,128,128]{0,2,1:T(8,128)S(1)}, u32[]{:S(2)}) copy-start(f32[256,128,128]{0,2,1:T(8,128)S(1)} %fusion.28) | copy-start | bytes 50331652
  20.8 23.1 %collective-permute-start.2 = (f32[256,1,128]{0,2,1:T(8,128)S(1)}, f32[256,1,128]{0,2,1:T(8,128)S(1)}, u32[]{:S(2)}, u32[]{:S(2)}) collective-permute-start(f32[256,1,128]{0,2,1:T(8,128)S(1)} %get-tuple-element.42), channel_id=1, source_target_pairs={{0,4},{4,8},{8,12},{12,16},{16,20},{20,24},{24,28},{1,5},{5,9},{9,... | collective-permute-start | bytes 393224 | tf_op jit(solution)/shard_map/ppermute | solution.py:24
  24.2 19.5 %copy-start.14 = (s32[128,128]{1,0:T(8,128)S(1)}, s32[128,128]{1,0:T(8,128)}, u32[]{:S(2)}) copy-start(s32[128,128]{1,0:T(8,128)} %param.13) | copy-start | bytes 196612
  24.2 19.5 %copy-start.15 = (f32[8]{0:T(128)S(1)}, f32[8]{0:T(128)}, u32[]{:S(2)}) copy-start(f32[8]{0:T(128)} %param.15) | copy-start | bytes 100
  24.3 19.7 %collective-permute-start.3 = (f32[256,1,128]{0,2,1:T(8,128)S(1)}, f32[256,1,128]{0,2,1:T(8,128)S(1)}, u32[]{:S(2)}, u32[]{:S(2)}) collective-permute-start(f32[256,1,128]{0,2,1:T(8,128)S(1)} %get-tuple-element.41), channel_id=1, source_target_pairs={{4,0},{8,4},{12,8},{16,12},{20,16},{24,20},{28,24},{5,1},{9,5},{13... | collective-permute-start | bytes 393224 | tf_op jit(solution)/shard_map/ppermute | solution.py:25
  44.1 5.2 collective-permute-start.4
  45.4 4.7 collective-permute-start.5
  81.5 5.7 copy-start
  340.7 4.8 collective-permute-start.6
  344.1 5.6 collective-permute-start.7
  355.9 7.7 %collective-permute-start.8 = (f32[32,130,1]{1,0,2:T(8,128)S(1)}, f32[32,130,1]{1,0,2:T(8,128)S(1)}, u32[]{:S(2)}, u32[]{:S(2)}) collective-permute-start(f32[32,130,1]{1,0,2:T(8,128)S(1)} %copy.48), channel_id=1, source_target_pairs={{1,0},{2,1},{3,2},{5,4},{6,5},{7,6},{9,8},{10,9},{11,10},{13,12},{... | collective-permute-start | bytes 49928 | tf_op jit(solution)/shard_map/ppermute | solution.py:25
  360.4 6.8 collective-permute-start.9
  375.4 1.3 copy-start.10
  433.7 17.9 %copy-start.8 = (f32[32,128,128]{2,0,1:T(8,128)S(1)}, f32[32,128,128]{2,0,1:T(8,128)}, u32[]{:S(2)}) copy-start(f32[32,128,128]{2,0,1:T(8,128)} %get-tuple-element.59) | copy-start | bytes 6291460
  451.5 59.9 %copy-start.2 = (f32[32,128,128]{2,0,1:T(8,128)}, f32[32,128,128]{2,0,1:T(8,128)S(1)}, u32[]{:S(2)}) copy-start(f32[32,128,128]{2,0,1:T(8,128)S(1)} %fusion.76) | copy-start | bytes 6291460
  513.9 1.4 copy-start.4
  515.2 5.7 collective-permute-start.10
  519.4 5.6 collective-permute-start.11
  531.2 7.6 %collective-permute-start.12 = (f32[32,130,1]{1,0,2:T(8,128)S(1)}, f32[32,130,1]{1,0,2:T(8,128)S(1)}, u32[]{:S(2)}, u32[]{:S(2)}) collective-permute-start(f32[32,130,1]{1,0,2:T(8,128)S(1)} %copy.53), channel_id=1, source_target_pairs={{1,0},{2,1},{3,2},{5,4},{6,5},{7,6},{9,8},{10,9},{11,10},{13,12},{... | collective-permute-start | bytes 49928 | tf_op jit(solution)/shard_map/ppermute | solution.py:25
  535.7 6.6 collective-permute-start.13
  550.5 16.5 %copy-start.9 = (f32[32,128,128]{2,0,1:T(8,128)}, f32[32,128,128]{2,0,1:T(8,128)S(1)}, u32[]{:S(2)}) copy-start(f32[32,128,128]{2,0,1:T(8,128)S(1)} %fusion.51) | copy-start | bytes 6291460
  550.5 57.5 %copy-start.3 = (f32[32,128,128]{2,0,1:T(8,128)S(1)}, f32[32,128,128]{2,0,1:T(8,128)}, u32[]{:S(2)}) copy-start(f32[32,128,128]{2,0,1:T(8,128)} %copy-done.2) | copy-start | bytes 6291460
  608.0 17.9 %copy-start.5 = (f32[32,128,128]{2,0,1:T(8,128)S(1)}, f32[32,128,128]{2,0,1:T(8,128)}, u32[]{:S(2)}) copy-start(f32[32,128,128]{2,0,1:T(8,128)} %copy-done.4) | copy-start | bytes 6291460
  608.0 17.9 %copy-start.16 = (f32[32,128,128]{2,0,1:T(8,128)S(1)}, f32[32,128,128]{2,0,1:T(8,128)}, u32[]{:S(2)}) copy-start(f32[32,128,128]{2,0,1:T(8,128)} %get-tuple-element.61) | copy-start | bytes 6291460
  625.9 18.9 %copy-start.7 = (f32[32,128,128]{2,0,1:T(8,128)}, f32[32,128,128]{2,0,1:T(8,128)S(1)}, u32[]{:S(2)}) copy-start(f32[32,128,128]{2,0,1:T(8,128)S(1)} %multiply_add_fusion.1) | copy-start | bytes 6291460
  625.9 58.3 %copy-start.6 = (f32[32,128,128]{2,0,1:T(8,128)S(1)}, f32[32,128,128]{2,0,1:T(8,128)}, u32[]{:S(2)}) copy-start(f32[32,128,128]{2,0,1:T(8,128)} %copy-done.4) | copy-start | bytes 6291460
  686.4 2.6 copy-start.17
  686.4 2.6 copy-start.18
Sparse Core Ops, SparseCore 0:
  125.8 132.1 all-reduce.4
where the time goes:
time: 722 us; the launch traced here: 716 us
  blocking collectives  205 us (28%)
  matrix products  203 us (28%)
  other arithmetic  108 us (15%)
  waiting for transfers between devices  96.4 us (13%)
  local copies, waits for them, and re-layouts  51.1 us (7%)
  starting transfers between devices  35.9 us (5%)
  between operations  16.7 us (2%)
    psum x1, waiting for transfers between devices, body(): inverse = invert(lax.psum(partial_matrix, ('row', 'col')))  87.1 us
    psum x2, blocking collectives, refresh(): projected = lax.psum(project(field_image), ('row', 'col'))  81 us
    dot_general x3, matrix products, expand(): jnp.dot(coarse, basis_flat, precision=precise)  56.2 us
    dot_general x3, matrix products, correction_image(): jnp.dot(coarse, image_flat, precision=precise)  54.2 us
    dot_general x3, matrix products, project(): lax.dot_general(field.reshape(load_count, tile_cells), basis_flat, contra...  51 us
    psum x1, blocking collectives, body(): load_sums = lax.psum(project(load_currents), ('row', 'col'))  45.2 us
    sub x3, other arithmetic, stencil(): diagonal * centre - right_link * padded[:, 1:-1, 2:]  40.6 us
    psum x1, blocking collectives, refresh(): weighted_norm = lax.psum(local_norm, ('row', 'col'))  39.8 us
  transfers between devices with their start and end apart: 15, of which 5 were waited for; matrix products, arithmetic and copies ran while one was open for 5% of the time, Pallas kernels for 0%

commit v1 on v0

--- a/solution.py
+++ b/solution.py
@@ -108,7 +108,9 @@
         local_norm = jnp.sum(residual * scaled, axis=(1, 2))
         field_image = stencil(extended(scaled, (("row", 1), ("col", 2)), 1), coeffs)
         weighted_norm = lax.psum(local_norm, ("row", "col"))
-        projected = lax.psum(project(field_image), ("row", "col"))
+        block = project(field_image)
+        blocks = lax.all_gather(block, ("row", "col"))
+        projected = jnp.sum(blocks, axis=0)
         coarse = jnp.dot(projected, inverse, precision=precise)
         return (scaled, weighted_norm, field_image, coarse)
 

time: 722 us -> 752 us (1.042)
  waiting for transfers between devices: 96.4 us -> 163 us
  blocking collectives: 205 us -> 164 us
    psum x2 -> x0, blocking collectives: 81 us -> none  [refresh(): projected = lax.psum(project(field_image), ('row', 'col'))]
    all_gather x0 -> x2, waiting for transfers between devices: none -> 66.5 us  [refresh(): blocks = lax.all_gather(block, ('row', 'col'))]
    psum x1 -> x2, blocking collectives: 39.8 us -> 79.5 us  [refresh(): weighted_norm = lax.psum(local_norm, ('row', 'col'))]
  transfers between devices with their start and end apart: 15 -> 17, of which waited for: 5 -> 7; matrix products, arithmetic and copies ran while one was open for 5% -> 5% of each run, Pallas kernels for 0% -> 0%
where the time goes in v1:
time: 752 us; the launch traced here: 746 us
  matrix products  204 us (27%)
  blocking collectives  164 us (22%)
  waiting for transfers between devices  163 us (22%)
  other arithmetic  111 us (15%)
  local copies, waits for them, and re-layouts  52.4 us (7%)
  starting transfers between devices  35.9 us (5%)
  between operations  16.3 us (2%)
    psum x1, waiting for transfers between devices, body(): inverse = invert(lax.psum(partial_matrix, ('row', 'col')))  87.1 us
    psum x2, blocking collectives, refresh(): weighted_norm = lax.psum(local_norm, ('row', 'col'))  79.5 us
    all_gather x2, waiting for transfers between devices, refresh(): blocks = lax.all_gather(block, ('row', 'col'))  66.5 us
    dot_general x3, matrix products, expand(): jnp.dot(coarse, basis_flat, precision=precise)  56.2 us
    dot_general x3, matrix products, correction_image(): jnp.dot(coarse, image_flat, precision=precise)  54.2 us
    dot_general x3, matrix products, project(): lax.dot_general(field.reshape(load_count, tile_cells), basis_flat, contra...  52.1 us
    psum x1, blocking collectives, body(): load_sums = lax.psum(project(load_currents), ('row', 'col'))  45.2 us
    sub x3, other arithmetic, stencil(): diagonal * centre - right_link * padded[:, 1:-1, 2:]  40.6 us
  transfers between devices with their start and end apart: 17, of which 7 were waited for; matrix products, arithmetic and copies ran while one was open for 5% of the time, Pallas kernels for 0%

profile of v1, /device:TPU:0, one launch (start us, length us, event | category | flops | bytes accessed | tf_op | source)
XLA Modules:
  0.0 746.2 jit_solution(12452373309344205350)
XLA Ops:
  8.4 2.4 collective-permute-start
  11.0 4.4 collective-permute-start.1
  15.3 5.4 fusion.28
  20.8 3.4 collective-permute-start.2
  24.3 1.4 collective-permute-start.3
  25.7 18.0 %fusion.84 = f32[32,256]{1,0:T(8,128)S(1)} fusion(f32[32,128,128]{2,1,0:T(8,128)S(1)} %copy-done.11, f32[128,128]{1,0:T(8,128)S(1)} %copy-done.12, s32[128,128]{1,0:T(8,128)S(1)} %copy-done.13), kind=kOutput, calls=%fused_computation.114 | convolution fusion | flops 1619001344 | bytes 2260992 | tf_op jit(solution)/shard_map/dot_general | solution.py:92
  44.1 1.3 collective-permute-start.4
  45.4 3.8 collective-permute-start.5
  50.1 31.3 %fusion.17 = f32[256,128,128]{0,2,1:T(8,128)S(1)} fusion(f32[256,128,128]{0,2,1:T(8,128)} %copy-done.1, f32[256,1,128]{0,2,1:T(8,128)S(1)} %collective-permute-done.2, f32[256,1,128]{0,2,1:T(8,128)S(1)} %collective-permute-done.3, f32[256,130,1]{0,2,1:T(1,128)S(1)} %collective-permute-done.5, f32[256,130,1]{0,2,1:T(1,128)S(1)} %collective-permute-done.4, ...), kind=kLoop, calls=%fused_computation.20 | loop fusion | flops 79691776 | bytes 34541568 | tf_op jit(solution)/shard_map/sub | solution.py:39
  81.5 5.7 copy-done
  87.2 38.4 %fusion.81 = f32[256,256]{0,1:T(8,128)} fusion(f32[256,128,128]{0,2,1:T(8,128)S(1)} %fusion.17, f32[128,128]{1,0:T(8,128)S(1)} %copy-done.12, s32[128,128]{1,0:T(8,128)S(1)} %copy-done.13), kind=kOutput, calls=%fused_computation.110 | convolution fusion | flops 12893290496 | bytes 17170432 | tf_op jit(solution)/shard_map/dot_general | solution.py:88
  125.7 45.2 %psum.42 = f32[32,256]{1,0:T(8,128)S(1)} all-reduce(f32[32,256]{1,0:T(8,128)S(1)} %fusion.84), channel_id=1, replica_groups=mesh['row'=8,'col'=4] {'row','col'}, use_global_device_ids=true, to_apply=%region_0.1 | all-reduce | flops 8192 | bytes 65536 | tf_op jit(solution)/shard_map/psum | solution.py:117
  171.0 87.1 %all-reduce.4.cloned.1.call-done = f32[256,256]{0,1:T(8,128)} async-done(((f32[256,256]{0,1:T(8,128)}), f32[256,256]{0,1:T(8,128)}) %all-reduce.4.cloned.1.call-update) | async-done | bytes 262160 | tf_op jit(solution)/shard_map/psum | solution.py:89
  258.1 1.1 copy.48
  260.1 11.7 %cholesky.53 = f32[128,128]{1,0:T(8,128)S(1)} custom-call(f32[128,128]{1,0:T(8,128)S(1)} %cholesky.121), custom_call_target="Cholesky" | custom-call | tf_op jit(solution)/shard_map/jit(cholesky)/cholesky | solution.py:48
  271.9 9.8 %custom-call.16 = f32[1,128,128]{1,2,0:T(8,128)S(1)} custom-call(f32[1,128,128]{2,1,0:T(8,128)S(1)} %get-tuple-element.54), custom_call_target="InvertDiagBlocksLowerTriangular" | custom-call | tf_op jit(solution)/shard_map/jit(cholesky)/cholesky | solution.py:48
  282.2 11.7 %cholesky.108 = f32[128,128]{1,0:T(8,128)S(1)} custom-call(f32[128,128]{1,0:T(8,128)S(1)} %convolution_subtract_fusion.2), custom_call_target="Cholesky" | custom-call | tf_op jit(solution)/shard_map/jit(cholesky)/cholesky | solution.py:48
  296.1 4.1 while.1
  296.7 1.4 bitcast_dynamic-update-slice_fusion.2
  298.8 1.4 bitcast_dynamic-update-slice_fusion.2
  300.2 20.1 %custom-call.17 = f32[2,128,128]{1,2,0:T(8,128)S(1)} custom-call(f32[2,128,128]{2,1,0:T(8,128)S(1)} %get-tuple-element.9), custom_call_target="InvertDiagBlocksLowerTriangular" | custom-call | tf_op jit(solution)/shard_map/triangular_solve | solution.py:51
  322.3 18.5 %multiply_reduce_fusion.3 = (f32[32]{0:T(128)S(1)}, f32[32,128,128]{2,0,1:T(8,128)S(1)}, f32[32,128,128]{2,0,1:T(8,128)}) fusion(f32[128,128]{1,0:T(8,128)S(1)} %get-tuple-element.32, f32[32,256,1]{1,0,2:T(8,128)S(1)} %convolution_bitcast_fusion.2, f32[256,128,128]{0,2,1:T(8,128)} %copy-done, f32[32,128,128]{2,1,0:T(8,128)} %param.8), kind=kOutput, calls=%fused_computation.105 | convolution fusion | flops 1612709888 | bytes 23167104 | tf_op jit(solution)/shard_map/dot_general | solution.py:102
  340.8 3.4 collective-permute-start.6
  344.2 1.3 collective-permute-start.7
  345.6 4.2 collective-permute-done.7
  350.0 2.7 fusion.119
  352.7 3.2 copy.50
  355.9 1.3 collective-permute-start.8
  357.2 3.2 copy.52
  360.4 3.2 collective-permute-start.9
  363.6 3.6 copy.51
  367.2 3.6 copy.53
  370.8 4.6 fusion.59
  375.4 1.3 copy-done.10
  376.7 17.0 %fusion.89 = f32[32,256]{1,0:T(8,128)} fusion(f32[32,128,128]{2,0,1:T(8,128)S(1)} %fusion.59, f32[128,128]{1,0:T(8,128)S(1)} %copy-done.12, s32[128,128]{1,0:T(8,128)S(1)} %copy-done.13), kind=kOutput, calls=%fused_computation.115 | convolution fusion | flops 1619001344 | bytes 2260992 | tf_op jit(solution)/shard_map/dot_general | solution.py:92
  393.8 53.6 %all-gather.5.cloned.1.call-done = f32[1024,256]{1,0:T(8,128)} async-done(((f32[32,256]{1,0:T(8,128)}), f32[1024,256]{1,0:T(8,128)}) %all-gather.5.cloned.1.call-update) | async-done | bytes 1048592 | tf_op jit(solution)/shard_map/all_gather | solution.py:112
  447.4 1.3 reduce_sum.85
  449.0 17.8 %fusion.76 = f32[32,128,128]{2,0,1:T(8,128)S(1)} fusion(f32[32,128,128]{2,0,1:T(8,128)} %copy-done.10, f32[32,256,1]{1,0,2:T(8,128)S(1)} %convolution_bitcast_fusion.1, f32[256,128,128]{0,2,1:T(8,128)} %copy-done), kind=kOutput, calls=%fused_computation.109 | convolution fusion | flops 1611137024 | bytes 21004288 | tf_op jit(solution)/shard_map/dot_general | solution.py:102
  466.9 20.1 %multiply_reduce_fusion.2 = (f32[32]{0:T(128)S(1)}, f32[32,128,128]{2,0,1:T(8,128)}) fusion(f32[32,128,128]{2,0,1:T(8,128)S(1)} %fusion.76, f32[32,256,1]{1,0,2:T(8,128)S(1)} %convolution_bitcast_fusion.1, f32[128,128]{1,0:T(8,128)S(1)} %copy-done.12, s32[128,128]{1,0:T(8,128)S(1)} %copy-done.13, f32[32,128,128]{2,0,1:T(8,128)S(1)} %copy-done.8, ...), kind=kOutput, calls=%fused_computation.104 | convolution fusion | flops 1621098496 | bytes 6520960 | tf_op jit(solution)/shard_map/dot_general | solution.py:97
  486.9 39.3 %all-reduce.1 = (f32[32]{0:T(128)S(1)}, f32[32]{0:T(128)S(1)}) all-reduce(f32[32]{0:T(128)S(1)} %get-tuple-element.41, f32[32]{0:T(128)S(1)} %get-tuple-element.58), channel_id=1, replica_groups=mesh['row'=8,'col'=4] {'row','col'}, use_global_device_ids=true, to_apply=%region_10.11 | all-reduce | flops 64 | bytes 512 | tf_op jit(solution)/shard_map/psum | solution.py:110
  526.2 2.4 multiply_reduce_fusion.1
  530.0 4.2 collective-permute-start.10
  534.2 1.5 collective-permute-start.11
  535.7 4.1 collective-permute-done.11
  540.0 2.7 fusion.118
  542.7 3.2 copy.55
  545.9 1.3 collective-permute-start.12
  547.2 3.2 copy.57
  550.4 3.0 collective-permute-start.13
  553.5 3.6 copy.56
  557.0 3.6 copy.58
  560.6 4.6 fusion.51
  565.3 1.3 copy-done.9
  566.6 17.0 %fusion.92 = f32[32,256]{1,0:T(8,128)} fusion(f32[32,128,128]{2,0,1:T(8,128)S(1)} %fusion.51, f32[128,128]{1,0:T(8,128)S(1)} %copy-done.12, s32[128,128]{1,0:T(8,128)S(1)} %copy-done.13), kind=kOutput, calls=%fused_computation.116 | convolution fusion | flops 1619001344 | bytes 2260992 | tf_op jit(solution)/shard_map/dot_general | solution.py:92
  583.6 40.2 %psum.46 = f32[32]{0:T(128)S(1)} all-reduce(f32[32]{0:T(128)S(1)} %get-tuple-element.30), channel_id=1, replica_groups=mesh['row'=8,'col'=4] {'row','col'}, use_global_device_ids=true, to_apply=%region_15.16 | all-reduce | flops 32 | bytes 256 | tf_op jit(solution)/shard_map/psum | solution.py:110
  623.8 12.8 %all-gather.7.cloned.1.call-done = f32[1024,256]{1,0:T(8,128)} async-done(((f32[32,256]{1,0:T(8,128)}), f32[1024,256]{1,0:T(8,128)}) %all-gather.7.cloned.1.call-update) | async-done | bytes 1048592 | tf_op jit(solution)/shard_map/all_gather | solution.py:112
  636.6 1.3 reduce_sum.88
  638.2 17.9 %multiply_add_fusion.1 = f32[32,128,128]{2,0,1:T(8,128)S(1)} fusion(f32[32,128,128]{2,0,1:T(8,128)S(1)} %copy-done.3, f32[32,128,128]{2,0,1:T(8,128)} %copy-done.9, f32[32,256,1]{1,0,2:T(8,128)S(1)} %convolution_bitcast_fusion, f32[256,128,128]{0,2,1:T(8,128)} %copy-done, f32[32]{0:T(128)S(1)} %div.37), kind=kOutput, calls=%fused_computation.100 | convolution fusion | flops 1612185600 | bytes 23101568 | tf_op jit(solution)/shard_map/dot_general | solution.py:102
  656.1 18.9 %multiply_reduce_fusion = (f32[32]{0:T(128)S(1)}, f32[32,128,128]{2,0,1:T(8,128)}) fusion(f32[32,128,128]{2,0,1:T(8,128)S(1)} %multiply_add_fusion.1, f32[32,128,128]{2,0,1:T(8,128)S(1)} %copy-done.16, f32[32]{0:T(128)S(1)} %div.37, f32[32,256,1]{1,0,2:T(8,128)S(1)} %convolution_bitcast_fusion, f32[128,128]{1,0:T(8,128)S(1)} %copy-done.12, ...), kind=kOutput, calls=%fused_computation.99 | convolution fusion | flops 1622147072 | bytes 8618240 | tf_op jit(solution)/shard_map/dot_general | solution.py:97
  675.0 39.7 %psum.47 = f32[32]{0:T(128)S(1)} all-reduce(f32[32]{0:T(128)S(1)} %get-tuple-element.60), channel_id=1, replica_groups=mesh['row'=8,'col'=4] {'row','col'}, use_global_device_ids=true, to_apply=%region_18.19 | all-reduce | flops 32 | bytes 256 | tf_op jit(solution)/shard_map/psum | solution.py:127
  714.7 2.1 multiply_subtract_fusion
  716.8 2.5 copy.61
  719.4 17.3 %multiply_add_fusion = f32[32,128,128]{2,0,1:T(8,128)S(1)} fusion(f32[32,128,128]{2,0,1:T(8,128)S(1)} %copy-done.18, f32[32,128,128]{2,0,1:T(8,128)S(1)} %copy-done.17, f32[32,256,1]{1,0,2:T(8,128)S(1)} %convolution_bitcast_fusion.2, f32[128,128]{1,0:T(8,128)S(1)} %copy-done.12, s32[128,128]{1,0:T(8,128)S(1)} %copy-done.13, f32[32]{0:T(128)S(1)} %div.38, ...), kind=kOutput, calls=%fused_computation.98 | convolution fusion | flops 1621098496 | bytes 6455552 | tf_op jit(solution)/shard_map/dot_general | solution.py:97
  736.6 2.5 copy.60
  (98 shorter events, 10.6 us)
Async XLA Ops:
  7.2 250.9 %all-reduce.4.cloned.1.call-start = ((), (), s32[]{:S(2)}) async-start(), calls=%async_computation | async-start | bytes 524288 | tf_op jit(solution)/shard_map/psum | solution.py:89
  8.4 40.8 %collective-permute-start = (f32[128,1]{1,0:T(8,128)S(1)}, f32[128,1]{1,0:T(8,128)S(1)}, u32[]{:S(2)}, u32[]{:S(2)}) collective-permute-start(f32[128,1]{1,0:T(8,128)S(1)} %slice.188), channel_id=1, source_target_pairs={{0,1},{1,2},{2,3},{4,5},{5,6},{6,7},{8,9},{9,10},{10,11},{12,13},{... | collective-permute-start | bytes 1544 | tf_op jit(solution)/shard_map/ppermute | solution.py:14
  10.9 14.8 %copy-start.11 = (f32[32,128,128]{2,1,0:T(8,128)S(1)}, f32[32,128,128]{2,1,0:T(8,128)}, u32[]{:S(2)}) copy-start(f32[32,128,128]{2,1,0:T(8,128)} %param.8) | copy-start | bytes 6291460
  10.9 14.8 %copy-start.12 = (f32[128,128]{1,0:T(8,128)S(1)}, f32[128,128]{1,0:T(8,128)}, u32[]{:S(2)}) copy-start(f32[128,128]{1,0:T(8,128)} %param.10) | copy-start | bytes 196612
  10.9 14.8 %copy-start.13 = (s32[128,128]{1,0:T(8,128)S(1)}, s32[128,128]{1,0:T(8,128)}, u32[]{:S(2)}) copy-start(s32[128,128]{1,0:T(8,128)} %param.9) | copy-start | bytes 196612
  11.0 38.2 %collective-permute-start.1 = (f32[1,128]{1,0:T(1,128)S(1)}, f32[1,128]{1,0:T(1,128)S(1)}, u32[]{:S(2)}, u32[]{:S(2)}) collective-permute-start(f32[1,128]{1,0:T(1,128)S(1)} %slice.190), channel_id=1, source_target_pairs={{0,4},{4,8},{8,12},{12,16},{16,20},{20,24},{24,28},{1,5},{5,9},{9,... | collective-permute-start | bytes 1544 | tf_op jit(solution)/shard_map/ppermute | solution.py:14
  20.7 23.2 %copy-start.1 = (f32[256,128,128]{0,2,1:T(8,128)}, f32[256,128,128]{0,2,1:T(8,128)S(1)}, u32[]{:S(2)}) copy-start(f32[256,128,128]{0,2,1:T(8,128)S(1)} %fusion.28) | copy-start | bytes 50331652
  20.8 23.1 %collective-permute-start.2 = (f32[256,1,128]{0,2,1:T(8,128)S(1)}, f32[256,1,128]{0,2,1:T(8,128)S(1)}, u32[]{:S(2)}, u32[]{:S(2)}) collective-permute-start(f32[256,1,128]{0,2,1:T(8,128)S(1)} %get-tuple-element.40), channel_id=1, source_target_pairs={{0,4},{4,8},{8,12},{12,16},{16,20},{20,24},{24,28},{1,5},{5,9},{9,... | collective-permute-start | bytes 393224 | tf_op jit(solution)/shard_map/ppermute | solution.py:24
  24.2 19.5 %copy-start.14 = (s32[128,128]{1,0:T(8,128)S(1)}, s32[128,128]{1,0:T(8,128)}, u32[]{:S(2)}) copy-start(s32[128,128]{1,0:T(8,128)} %param.13) | copy-start | bytes 196612
  24.2 19.5 %copy-start.15 = (f32[8]{0:T(128)S(1)}, f32[8]{0:T(128)}, u32[]{:S(2)}) copy-start(f32[8]{0:T(128)} %param.15) | copy-start | bytes 100
  24.3 19.7 %collective-permute-start.3 = (f32[256,1,128]{0,2,1:T(8,128)S(1)}, f32[256,1,128]{0,2,1:T(8,128)S(1)}, u32[]{:S(2)}, u32[]{:S(2)}) collective-permute-start(f32[256,1,128]{0,2,1:T(8,128)S(1)} %get-tuple-element.39), channel_id=1, source_target_pairs={{4,0},{8,4},{12,8},{16,12},{20,16},{24,20},{28,24},{5,1},{9,5},{13... | collective-permute-start | bytes 393224 | tf_op jit(solution)/shard_map/ppermute | solution.py:25
  44.1 5.2 collective-permute-start.4
  45.4 4.7 collective-permute-start.5
  81.5 5.7 copy-start
  125.7 321.8 %all-gather.5.cloned.1.call-start = ((), (), s32[]{:S(2)}) async-start(), calls=%async_computation.1 | async-start | bytes 1081344 | tf_op jit(solution)/shard_map/all_gather | solution.py:112
  340.8 4.8 collective-permute-start.6
  344.2 5.6 collective-permute-start.7
  355.9 7.7 %collective-permute-start.8 = (f32[32,130,1]{1,0,2:T(8,128)S(1)}, f32[32,130,1]{1,0,2:T(8,128)S(1)}, u32[]{:S(2)}, u32[]{:S(2)}) collective-permute-start(f32[32,130,1]{1,0,2:T(8,128)S(1)} %copy.50), channel_id=1, source_target_pairs={{1,0},{2,1},{3,2},{5,4},{6,5},{7,6},{9,8},{10,9},{11,10},{13,12},{... | collective-permute-start | bytes 49928 | tf_op jit(solution)/shard_map/ppermute | solution.py:25
  360.4 6.8 collective-permute-start.9
  375.4 1.3 copy-start.10
  393.8 242.9 %all-gather.7.cloned.1.call-start = ((), (), s32[]{:S(2)}) async-start(), calls=%async_computation.2 | async-start | bytes 1081344 | tf_op jit(solution)/shard_map/all_gather | solution.py:112
  449.0 17.9 %copy-start.8 = (f32[32,128,128]{2,0,1:T(8,128)S(1)}, f32[32,128,128]{2,0,1:T(8,128)}, u32[]{:S(2)}) copy-start(f32[32,128,128]{2,0,1:T(8,128)} %get-tuple-element.57) | copy-start | bytes 6291460
  466.8 59.4 %copy-start.2 = (f32[32,128,128]{2,0,1:T(8,128)}, f32[32,128,128]{2,0,1:T(8,128)S(1)}, u32[]{:S(2)}) copy-start(f32[32,128,128]{2,0,1:T(8,128)S(1)} %fusion.76) | copy-start | bytes 6291460
  528.6 1.4 copy-start.4
  530.0 5.7 collective-permute-start.10
  534.2 5.6 collective-permute-start.11
  545.9 7.6 %collective-permute-start.12 = (f32[32,130,1]{1,0,2:T(8,128)S(1)}, f32[32,130,1]{1,0,2:T(8,128)S(1)}, u32[]{:S(2)}, u32[]{:S(2)}) collective-permute-start(f32[32,130,1]{1,0,2:T(8,128)S(1)} %copy.55), channel_id=1, source_target_pairs={{1,0},{2,1},{3,2},{5,4},{6,5},{7,6},{9,8},{10,9},{11,10},{13,12},{... | collective-permute-start | bytes 49928 | tf_op jit(solution)/shard_map/ppermute | solution.py:25
  550.4 6.6 collective-permute-start.13
  565.3 1.3 copy-start.9
  566.6 71.6 %copy-start.3 = (f32[32,128,128]{2,0,1:T(8,128)S(1)}, f32[32,128,128]{2,0,1:T(8,128)}, u32[]{:S(2)}) copy-start(f32[32,128,128]{2,0,1:T(8,128)} %copy-done.2) | copy-start | bytes 6291460
  638.2 17.9 %copy-start.5 = (f32[32,128,128]{2,0,1:T(8,128)S(1)}, f32[32,128,128]{2,0,1:T(8,128)}, u32[]{:S(2)}) copy-start(f32[32,128,128]{2,0,1:T(8,128)} %copy-done.4) | copy-start | bytes 6291460
  638.2 17.9 %copy-start.16 = (f32[32,128,128]{2,0,1:T(8,128)S(1)}, f32[32,128,128]{2,0,1:T(8,128)}, u32[]{:S(2)}) copy-start(f32[32,128,128]{2,0,1:T(8,128)} %get-tuple-element.59) | copy-start | bytes 6291460
  656.1 18.9 %copy-start.7 = (f32[32,128,128]{2,0,1:T(8,128)}, f32[32,128,128]{2,0,1:T(8,128)S(1)}, u32[]{:S(2)}) copy-start(f32[32,128,128]{2,0,1:T(8,128)S(1)} %multiply_add_fusion.1) | copy-start | bytes 6291460
  656.1 58.6 %copy-start.6 = (f32[32,128,128]{2,0,1:T(8,128)S(1)}, f32[32,128,128]{2,0,1:T(8,128)}, u32[]{:S(2)}) copy-start(f32[32,128,128]{2,0,1:T(8,128)} %copy-done.4) | copy-start | bytes 6291460
  716.8 2.6 copy-start.17
  716.8 2.6 copy-start.18
Sparse Core Ops, SparseCore 0:
  125.8 132.2 all-reduce.3
  393.9 53.5 all-gather.4
  583.7 52.8 all-gather.6
